TPU v7x, 128 devices: a whole 4x4x4 slice. The times are simulated.
128 devices in a mesh: req: 4 (over x), tp: 32 (over z, y, core).
Axes of the slice: x: 4, y: 4, z: 4, core: 2. Of those that a mesh axis runs over, the one named last changes fastest.
Arguments:
- step_inputs: bfloat16 [4, 256, 1536], P(None, ('req', 'tp')), may hold values from -6 to 6
- qkv_weight: bfloat16 [1536, 2048], replicated, may hold values from -0.15625 to 0.15625
- qkv_bias: float32 [2048], replicated, may hold values from -8 to 8
- out_weight: bfloat16 [1536, 1536], P('tp'), may hold values from -0.15625 to 0.15625
- gate_weight: bfloat16 [1536, 8960], P(None, 'tp'), may hold values from -0.15625 to 0.15625
- up_weight: bfloat16 [1536, 8960], P(None, 'tp'), may hold values from -0.15625 to 0.15625
- down_weight: bfloat16 [8960, 1536], P('tp'), may hold values from -0.0625 to 0.0625
- cache_keys: bfloat16 [256, 4096, 256], P(('req', 'tp')), may hold values from -60 to 60
- cache_values: bfloat16 [256, 4096, 256], P(('req', 'tp')), may hold values from -24 to 24
- lengths: int32 [32, 8], replicated, may hold values from 1 to 4096, as said below
- parents: int32 [4, 32, 8], replicated, may hold values from 0 to 7
- slot_request: int32 [32], replicated, may hold values from 0 to 31, each once
Outputs:
- outputs: bfloat16 [4, 256, 1536], P(None, ('req', 'tp'))
Inputs may be any that keep to these rules, and one draw needn't show every extreme that they name: lengths[r, c] is the number of cached positions of beam c of request r; some beam has exactly 4096. parents[t, r, b] names a beam of the same request r. `slot_request`: a permutation of the requests; slots 8 * i to 8 * i + 7 are rows of index i of req.
All inputs are finite; a program needn't handle non-finite values.
Results may differ from a plain program's by a relative error of at most 0.022.
The roundings to bfloat16 on the way count: a program that leaves them out, or rounds other values in their place, can miss the bound.
Values may be sent and summed in bfloat16 or wider, within the bound.
No kernel may reach another device: no remote copies, remote signals or barrier semaphores. Data moves between devices by JAX's collectives and lax.ppermute only.
A program may use at most 128 MiB of HBM per device.

v0:
```python
import jax
import jax.numpy as jnp
from jax import lax
from jax.sharding import PartitionSpec as P

Q_HEADS = 12
KV_HEADS = 2
theta_base = 1000000.0
norm_eps = 1e-06
masked_score = -1e30


def rms_normed(values):
    values = values.astype(jnp.float32)
    factor = lax.rsqrt(jnp.mean(values * values, axis=-1, keepdims=True) + norm_eps)
    return (values * factor).astype(jnp.bfloat16)


def rotate(vectors, positions):
    half = vectors.shape[-1] // 2
    freqs = theta_base ** (-jnp.arange(half, dtype=jnp.float32) * 2.0 / vectors.shape[-1])
    angles = positions.astype(jnp.float32)[:, None] * freqs[None, :]
    cosine = jnp.cos(angles)[:, None, :]
    sine = jnp.sin(angles)[:, None, :]
    values = vectors.astype(jnp.float32)
    first = values[..., :half]
    second = values[..., half:]
    return jnp.concatenate(
        [first * cosine - second * sine, second * cosine + first * sine], axis=-1
    ).astype(jnp.bfloat16)


def owner_rows(flat, owned_count, beams, inverse):
    owned_global = flat * owned_count + jnp.arange(owned_count, dtype=jnp.int32)
    owned_request = owned_global // beams
    owned_beam = owned_global % beams
    beam_range = jnp.arange(beams, dtype=jnp.int32)
    query_rows = (inverse[owned_request][:, None] * beams + beam_range[None, :]).reshape(-1)
    return (owned_request, owned_beam, query_rows)


def owned_attention(
    every_query, keys, values, owned_request, owned_beam, query_rows, root_all, lengths
):
    owned_rows, context, kv_width = keys.shape
    beams = root_all.shape[1]
    head_dim = kv_width // KV_HEADS
    group = Q_HEADS // KV_HEADS
    grouped = jnp.take(every_query, query_rows, axis=0).reshape(
        owned_rows, beams, KV_HEADS, group, head_dim
    )
    keys = keys.reshape(owned_rows, context, KV_HEADS, head_dim)
    values = values.reshape(owned_rows, context, KV_HEADS, head_dim)
    scores = jnp.einsum(
        "jbkgd,jpkd->jbkgp", grouped, keys, preferred_element_type=jnp.float32
    ) * head_dim ** (-0.5)
    limits = lengths[owned_request, owned_beam]
    live = (jnp.arange(context, dtype=jnp.int32)[None, :] < limits[:, None])[:, None, None, None, :]
    scores = jnp.where(live, scores, masked_score)
    peak = jnp.max(scores, axis=-1)
    weights = jnp.where(live, jnp.exp(scores - peak[..., None]), 0.0)
    total = jnp.sum(weights, axis=-1)
    output = jnp.einsum(
        "jbkgp,jpkd->jbkgd",
        weights.astype(jnp.bfloat16),
        values,
        preferred_element_type=jnp.float32,
    )
    chosen = (root_all[owned_request] == owned_beam[:, None])[:, :, None, None]
    peak = jnp.where(chosen, peak, 0.0).reshape(owned_rows * beams, KV_HEADS, group)
    total = jnp.where(chosen, total, 0.0).reshape(owned_rows * beams, KV_HEADS, group)
    output = jnp.where(chosen[..., None], output, 0.0).reshape(
        owned_rows * beams, KV_HEADS, group, head_dim
    )
    return (peak, total, output)


def spread_rows(pieces, target_rows, row_count):
    return tuple(
        (
            jnp.zeros((row_count,) + piece.shape[1:], jnp.float32).at[target_rows].add(piece)
            for piece in pieces
        )
    )


def per_device(
    step_inputs,
    qkv_weight,
    qkv_bias,
    out_weight,
    gate_weight,
    up_weight,
    down_weight,
    cache_keys,
    cache_values,
    lengths,
    parents,
    slot_request,
):
    steps_count, rows_dev, width = step_inputs.shape
    beams = parents.shape[2]
    requests = slot_request.shape[0]
    req_count = lax.axis_size("req")
    tp_count = lax.axis_size("tp")
    group_requests = requests // req_count
    group_rows = group_requests * beams
    total_rows = requests * beams
    owned_count = cache_keys.shape[0]
    kv_width = cache_keys.shape[2]
    head_dim = kv_width // KV_HEADS
    group = Q_HEADS // KV_HEADS
    attn_width = Q_HEADS * head_dim
    req_index = lax.axis_index("req")
    tp_index = lax.axis_index("tp")
    flat_index = req_index * tp_count + tp_index
    my_requests = lax.dynamic_slice_in_dim(slot_request, req_index * group_requests, group_requests)
    inverse = (
        jnp.zeros((requests,), jnp.int32)
        .at[slot_request]
        .set(jnp.arange(requests, dtype=jnp.int32))
    )
    owned_request, owned_beam, query_rows = owner_rows(flat_index, owned_count, beams, inverse)
    beam_range = jnp.arange(beams, dtype=jnp.int32)
    root_all = jnp.broadcast_to(beam_range[None, :], (requests, beams))
    gen_keys = jnp.zeros((steps_count, group_rows, kv_width), jnp.bfloat16)
    gen_values = jnp.zeros((steps_count, group_rows, kv_width), jnp.bfloat16)
    base_rows = (jnp.arange(group_requests, dtype=jnp.int32) * beams)[:, None]
    column_width = out_weight.shape[0]
    results = []
    for step in range(steps_count):
        root_all = jnp.take_along_axis(root_all, parents[step], axis=1)
        reorder = (base_rows + parents[step][my_requests]).reshape(-1)
        gen_keys = jnp.take(gen_keys, reorder, axis=1)
        gen_values = jnp.take(gen_values, reorder, axis=1)
        inputs = step_inputs[step]
        normed = rms_normed(inputs)
        qkv = (
            jnp.dot(
                lax.all_gather(normed, "tp", axis=0, tiled=True),
                qkv_weight,
                preferred_element_type=jnp.float32,
            )
            + qkv_bias
        ).astype(jnp.bfloat16)
        my_roots = root_all[my_requests]
        positions = (jnp.take_along_axis(lengths[my_requests], my_roots, axis=1) + step).reshape(-1)
        queries = rotate(qkv[:, :attn_width].reshape(group_rows, Q_HEADS, head_dim), positions)
        new_keys = rotate(
            qkv[:, attn_width : attn_width + kv_width].reshape(group_rows, KV_HEADS, head_dim),
            positions,
        )
        gen_keys = gen_keys.at[step].set(new_keys.reshape(group_rows, kv_width))
        gen_values = gen_values.at[step].set(qkv[:, attn_width + kv_width :])
        every_query = lax.all_gather(
            queries.reshape(group_rows, attn_width), "req", axis=0, tiled=True
        )
        part_peak, part_total, part_output = owned_attention(
            every_query,
            cache_keys,
            cache_values,
            owned_request,
            owned_beam,
            query_rows,
            root_all,
            lengths,
        )
        all_peak, all_total, all_output = spread_rows(
            (part_peak, part_total, part_output), query_rows, total_rows
        )
        sum_peak, sum_total, sum_output = lax.psum((all_peak, all_total, all_output), ("req", "tp"))
        peak = lax.dynamic_slice_in_dim(sum_peak, req_index * group_rows, group_rows, 0)
        total = lax.dynamic_slice_in_dim(sum_total, req_index * group_rows, group_rows, 0)
        output = lax.dynamic_slice_in_dim(sum_output, req_index * group_rows, group_rows, 0)
        grouped = queries.reshape(group_rows, KV_HEADS, group, head_dim)
        past_keys = gen_keys[: step + 1].reshape(step + 1, group_rows, KV_HEADS, head_dim)
        past_values = gen_values[: step + 1].reshape(step + 1, group_rows, KV_HEADS, head_dim)
        recent_scores = jnp.einsum(
            "bkgd,sbkd->bkgs", grouped, past_keys, preferred_element_type=jnp.float32
        ) * head_dim ** (-0.5)
        top = jnp.maximum(peak, jnp.max(recent_scores, axis=-1))
        factor = jnp.exp(peak - top)
        recent_weights = jnp.exp(recent_scores - top[..., None])
        denominator = total * factor + jnp.sum(recent_weights, axis=-1)
        numerator = output * factor[..., None] + jnp.einsum(
            "bkgs,sbkd->bkgd",
            recent_weights.astype(jnp.bfloat16),
            past_values,
            preferred_element_type=jnp.float32,
        )
        attention = (
            (numerator / denominator[..., None])
            .reshape(group_rows, attn_width)
            .astype(jnp.bfloat16)
        )
        columns = lax.dynamic_slice_in_dim(attention, tp_index * column_width, column_width, 1)
        attended = lax.psum_scatter(
            jnp.dot(columns, out_weight, preferred_element_type=jnp.float32).astype(jnp.bfloat16),
            "tp",
            scatter_dimension=0,
            tiled=True,
        ).astype(jnp.float32)
        middle = inputs.astype(jnp.float32) + attended
        mixed_in = rms_normed(middle)
        piece = lax.all_gather(mixed_in, "tp", axis=0, tiled=True)
        gate = jnp.dot(piece, gate_weight, preferred_element_type=jnp.float32)
        upward = jnp.dot(piece, up_weight, preferred_element_type=jnp.float32)
        hidden = (jax.nn.silu(gate) * upward).astype(jnp.bfloat16)
        lowered = lax.psum_scatter(
            jnp.dot(hidden, down_weight, preferred_element_type=jnp.float32).astype(jnp.bfloat16),
            "tp",
            scatter_dimension=0,
            tiled=True,
        ).astype(jnp.float32)
        results.append((middle + lowered).astype(jnp.bfloat16))
    return jnp.stack(results)


def solution(mesh):
    in_specs = (
        P(None, ("req", "tp"), None),
        P(),
        P(),
        P("tp", None),
        P(None, "tp"),
        P(None, "tp"),
        P("tp", None),
        P(("req", "tp"), None, None),
        P(("req", "tp"), None, None),
        P(),
        P(),
        P(),
    )
    out_specs = P(None, ("req", "tp"), None)
    return jax.shard_map(
        per_device, mesh=mesh, in_specs=in_specs, out_specs=out_specs, check_vma=False
    )
```

profile of v0, /device:TPU:1, one launch (start us, length us, event | category | flops | bytes accessed | tf_op | source)
XLA Modules:
  0.0 1172.3 jit_solution(9988134711650191990)
XLA Ops:
  28.1 27.6 %all-gather = bf16[32,2,1536]{2,1,0:T(2,128)(2,1)S(1)} all-gather(bf16[1,2,1536]{2,1,0:T(2,128)(2,1)S(1)} %fusion.170), channel_id=1, replica_groups=mesh['req'=4,'tp'=32] {'tp'}, dimensions={0}, use_global_device_ids=true | all-gather | bytes 202752 | tf_op jit(solution)/shard_map/all_gather | solution.py:140
  55.8 4.0 fusion.28
  61.5 12.0 %all_gather.37 = bf16[256,1536]{1,0:T(8,128)(2,1)S(1)} all-gather(bf16[64,1536]{1,0:T(8,128)(2,1)S(1)} %bitcast.314), channel_id=1, replica_groups=mesh['req'=4,'tp'=32] {'req'}, dimensions={0}, use_global_device_ids=true | all-gather | bytes 983040 | tf_op jit(solution)/shard_map/all_gather | solution.py:155
  74.2 7.0 reshape.1079
  81.2 6.9 reshape.1080
  108.8 67.0 %all-reduce.9 = (f32[256,2,6]{0,1,2:T(2,128)S(1)}, f32[256,2,6]{0,1,2:T(2,128)S(1)}) all-reduce(f32[256,2,6]{0,1,2:T(2,128)S(1)} %copy.328, f32[256,2,6]{0,1,2:T(2,128)S(1)} %copy.335), channel_id=1, replica_groups=mesh['req'=4,'tp'=32] {'req','tp'}, use_global_device_ids=true, to_apply=%region_6.10 | all-reduce | flops 6144 | bytes 49152 | tf_op jit(solution)/shard_map/psum | solution.py:171
  185.9 63.2 %all-reduce.20.cloned.1.call-done = f32[256,2,6,128]{3,1,2,0:T(2,128)} async-done(((f32[256,2,6,128]{3,1,2,0:T(2,128)}), f32[256,2,6,128]{3,1,2,0:T(2,128)}) %all-reduce.20.cloned.1.call-update) | async-done | bytes 1572880 | tf_op jit(solution)/shard_map/psum | solution.py:171
  253.4 98.8 %all-reduce.22.cloned.1.call-done = bf16[64,1536]{1,0:T(8,128)(2,1)} async-done(((bf16[64,1536]{1,0:T(8,128)(2,1)}), bf16[64,1536]{1,0:T(8,128)(2,1)}) %all-reduce.22.cloned.1.call-update) | async-done | bytes 196624
  354.6 24.5 %all-gather.4 = bf16[32,2,1536]{2,1,0:T(2,128)(2,1)S(1)} all-gather(bf16[1,2,1536]{2,1,0:T(2,128)(2,1)S(1)} %get-tuple-element.172), channel_id=1, replica_groups=mesh['req'=4,'tp'=32] {'tp'}, dimensions={0}, use_global_device_ids=true | all-gather | bytes 202752 | tf_op jit(solution)/shard_map/all_gather | solution.py:140
  383.8 23.3 %all-gather.2 = bf16[32,2,1536]{2,1,0:T(2,128)(2,1)S(1)} all-gather(bf16[1,2,1536]{2,1,0:T(2,128)(2,1)S(1)} %get-tuple-element.171), channel_id=1, replica_groups=mesh['req'=4,'tp'=32] {'tp'}, dimensions={0}, use_global_device_ids=true | all-gather | bytes 202752 | tf_op jit(solution)/shard_map/all_gather | solution.py:140
  407.2 4.0 fusion.29
  414.6 23.7 %all-gather.6 = bf16[32,2,1536]{2,1,0:T(2,128)(2,1)S(1)} all-gather(bf16[1,2,1536]{2,1,0:T(2,128)(2,1)S(1)} %get-tuple-element.173), channel_id=1, replica_groups=mesh['req'=4,'tp'=32] {'tp'}, dimensions={0}, use_global_device_ids=true | all-gather | bytes 202752 | tf_op jit(solution)/shard_map/all_gather | solution.py:140
  438.5 4.0 fusion.31
  443.4 11.9 %all_gather.46 = bf16[256,1536]{1,0:T(8,128)(2,1)S(1)} all-gather(bf16[64,1536]{1,0:T(8,128)(2,1)S(1)} %bitcast.315), channel_id=1, replica_groups=mesh['req'=4,'tp'=32] {'req'}, dimensions={0}, use_global_device_ids=true | all-gather | bytes 983040 | tf_op jit(solution)/shard_map/all_gather | solution.py:155
  458.1 10.9 all_gather.40
  470.6 11.8 %all_gather.43 = bf16[256,1536]{1,0:T(8,128)(2,1)S(1)} all-gather(bf16[64,1536]{1,0:T(8,128)(2,1)S(1)} %bitcast.317), channel_id=1, replica_groups=mesh['req'=4,'tp'=32] {'req'}, dimensions={0}, use_global_device_ids=true | all-gather | bytes 983040 | tf_op jit(solution)/shard_map/all_gather | solution.py:155
  551.3 30.5 %all-gather.1 = bf16[32,2,1536]{2,1,0:T(2,128)(2,1)S(1)} all-gather(bf16[1,2,1536]{2,1,0:T(2,128)(2,1)S(1)} %copy-done.66), channel_id=1, replica_groups=mesh['req'=4,'tp'=32] {'tp'}, dimensions={0}, use_global_device_ids=true | all-gather | bytes 202752 | tf_op jit(solution)/shard_map/all_gather | solution.py:205
  588.9 119.1 %all-reduce.24.cloned.1.call-done = (f32[256,2,6]{2,1,0:T(2,128)}, f32[256,2,6]{2,1,0:T(2,128)}, f32[256,2,6]{2,1,0:T(2,128)}, f32[256,2,6]{2,1,0:T(2,128)}, f32[256,2,6]{2,1,0:T(2,128)}, /*index=5*/f32[256,2,6]{2,1,0:T(2,128)}) async-done(((f32[256,2,6]{2,1,0:T(2,128)}, f32[256,2,6]{2,1,0:T(2,128)}, f32[256,2,6]{2,1,0:T(2,128)}, f32[256,2,6]{2,1,0:T(2,128)}, f32[256,2,6]{2,1,0:T(2,128)}, ...) | async-done | bytes 73744 | tf_op jit(solution)/shard_map/psum | solution.py:171
  715.0 154.8 %all-reduce.26.cloned.1.call-done = (f32[256,2,6,128]{3,2,1,0:T(8,128)}, f32[256,2,6,128]{3,2,1,0:T(8,128)}, f32[256,2,6,128]{3,2,1,0:T(8,128)}) async-done(((f32[256,2,6,128]{3,2,1,0:T(8,128)}, f32[256,2,6,128]{3,2,1,0:T(8,128)}, f32[256,2,6,128]{3,2,1,0:T(8,128)}), (f32[256,2,6,128]{3,2,1,0:T(8,128)}, f32[256,2,6,128]{3,2,1,0:T(8,128)}, f32[256,2,6,128]{3,2,1,0:T(8,128)})) %all-reduce.26.cloned.1.call-update) | async-done | bytes 4718608 | tf_op jit(solution)/shard_map/psum | solution.py:171
  880.4 100.5 %all-reduce.30.cloned.1.call-done = (bf16[64,1536]{1,0:T(8,128)(2,1)}, bf16[64,1536]{1,0:T(8,128)(2,1)}, bf16[64,1536]{1,0:T(8,128)(2,1)}) async-done(((bf16[64,1536]{1,0:T(8,128)(2,1)}, bf16[64,1536]{1,0:T(8,128)(2,1)}, bf16[64,1536]{1,0:T(8,128)(2,1)}), (bf16[64,1536]{1,0:T(8,128)(2,1)}, bf16[64,1536]{1,0:T(8,128)(2,1)}, bf16[64,1536]{1,0:T(8,128)(2,1)})) %all-reduce.30.cloned.1.call-update) | async-done | bytes 589840
  982.8 24.9 %all-gather.3 = bf16[32,2,1536]{2,1,0:T(2,128)(2,1)S(1)} all-gather(bf16[1,2,1536]{2,1,0:T(2,128)(2,1)S(1)} %get-tuple-element.174), channel_id=1, replica_groups=mesh['req'=4,'tp'=32] {'tp'}, dimensions={0}, use_global_device_ids=true | all-gather | bytes 202752 | tf_op jit(solution)/shard_map/all_gather | solution.py:205
  1009.9 22.5 %all-gather.5 = bf16[32,2,1536]{2,1,0:T(2,128)(2,1)S(1)} all-gather(bf16[1,2,1536]{2,1,0:T(2,128)(2,1)S(1)} %get-tuple-element.176), channel_id=1, replica_groups=mesh['req'=4,'tp'=32] {'tp'}, dimensions={0}, use_global_device_ids=true | all-gather | bytes 202752 | tf_op jit(solution)/shard_map/all_gather | solution.py:205
  1034.5 24.1 %all-gather.7 = bf16[32,2,1536]{2,1,0:T(2,128)(2,1)S(1)} all-gather(bf16[1,2,1536]{2,1,0:T(2,128)(2,1)S(1)} %get-tuple-element.175), channel_id=1, replica_groups=mesh['req'=4,'tp'=32] {'tp'}, dimensions={0}, use_global_device_ids=true | all-gather | bytes 202752 | tf_op jit(solution)/shard_map/all_gather | solution.py:205
  1060.8 102.6 %all-reduce.28.cloned.1.call-done = (bf16[64,1536]{1,0:T(8,128)(2,1)}, bf16[64,1536]{1,0:T(8,128)(2,1)}, bf16[64,1536]{1,0:T(8,128)(2,1)}, bf16[64,1536]{1,0:T(8,128)(2,1)}) async-done(((bf16[64,1536]{1,0:T(8,128)(2,1)}, bf16[64,1536]{1,0:T(8,128)(2,1)}, bf16[64,1536]{1,0:T(8,128)(2,1)}, bf16[64,1536]{1,0:T(8,128)(2,1)}), (bf16[64,1536]{1,0:T(8,128)(2,1)}, bf16[64,1536]{1,0:T(8,128)(2,1)}, ...) | async-done | bytes 786448
  (502 shorter events, 176.0 us)
Async XLA Ops:
  6.5 872.2 %copy-start = (bf16[280,1536]{1,0:T(8,128)(2,1)S(1)}, bf16[280,1536]{1,0:T(8,128)(2,1)}, u32[]{:S(2)}) copy-start(bf16[280,1536]{1,0:T(8,128)(2,1)} %param.42) | copy-start | bytes 2580484
  6.5 242.6 %all-reduce.20.cloned.1.call-start = ((), (), s32[]{:S(2)}) async-start(), calls=%async_computation | async-start | bytes 3145728 | tf_op jit(solution)/shard_map/psum | solution.py:171
  8.8 79.9 %copy-start.68 = (pred[16]{0:T(512)(128)(4,1)}, pred[16]{0:T(512)(128)(4,1)S(1)}, u32[]{:S(2)}) copy-start(pred[16]{0:T(512)(128)(4,1)S(1)} %compare_and_fusion.4) | copy-start | bytes 52
  26.7 29.1 %copy-start.53 = (f32[2048]{0:T(1024)S(1)}, f32[2048]{0:T(1024)}, u32[]{:S(2)}) copy-start(f32[2048]{0:T(1024)} %param.38) | copy-start | bytes 24580
  61.0 20.2 %copy-start.42 = (f32[64,64]{1,0:T(8,128)}, f32[64,64]{1,0:T(8,128)S(1)}, u32[]{:S(2)}) copy-start(f32[64,64]{1,0:T(8,128)S(1)} %get-tuple-element.217) | copy-start | bytes 49156
  61.0 20.2 %copy-start.44 = (f32[64,64]{1,0:T(8,128)}, f32[64,64]{1,0:T(8,128)S(1)}, u32[]{:S(2)}) copy-start(f32[64,64]{1,0:T(8,128)S(1)} %get-tuple-element.218) | copy-start | bytes 49156
  98.5 253.7 %all-reduce.22.cloned.1.call-start = ((), (), s32[]{:S(2)}) async-start(), calls=%async_computation.1 | async-start | bytes 393216
  102.3 78.6 %copy-start.75 = (pred[2,8]{1,0:T(4,128)(4,1)S(1)}, pred[2,8]{1,0:T(4,128)(4,1)}, u32[]{:S(2)}) copy-start(pred[2,8]{1,0:T(4,128)(4,1)} %get-tuple-element.206) | copy-start | bytes 52
  102.3 79.1 %copy-start.73 = (pred[2,8]{1,0:T(4,128)(4,1)S(1)}, pred[2,8]{1,0:T(4,128)(4,1)}, u32[]{:S(2)}) copy-start(pred[2,8]{1,0:T(4,128)(4,1)} %get-tuple-element.208) | copy-start | bytes 52
  102.3 79.7 %copy-start.71 = (pred[2,8]{1,0:T(4,128)(4,1)S(1)}, pred[2,8]{1,0:T(4,128)(4,1)}, u32[]{:S(2)}) copy-start(pred[2,8]{1,0:T(4,128)(4,1)} %get-tuple-element.207) | copy-start | bytes 52
  102.3 80.3 %copy-start.79 = (u32[128]{0:T(128)S(1)}, u32[128]{0:T(128)}, u32[]{:S(2)}) copy-start(u32[128]{0:T(128)} %constant.501) | copy-start | bytes 1540
  107.5 144.8 %copy-start.9 = (bf16[48,1536]{1,0:T(8,128)(2,1)S(1)}, bf16[48,1536]{1,0:T(8,128)(2,1)}, u32[]{:S(2)}) copy-start(bf16[48,1536]{1,0:T(8,128)(2,1)} %param.39) | copy-start | bytes 442372
  253.3 454.6 %all-reduce.24.cloned.1.call-start = ((), (), s32[]{:S(2)}) async-start(), calls=%async_computation.2 | async-start | bytes 3145728 | tf_op jit(solution)/shard_map/psum | solution.py:171
  456.8 26.4 %copy-start.69 = (pred[16]{0:T(512)(128)(4,1)S(1)}, pred[16]{0:T(512)(128)(4,1)}, u32[]{:S(2)}) copy-start(pred[16]{0:T(512)(128)(4,1)} %copy-done.68) | copy-start | bytes 52
  499.4 17.5 %copy-start.55 = (bf16[1,64,256]{2,1,0:T(8,128)(2,1)S(1)}, bf16[1,64,256]{2,1,0:T(8,128)(2,1)}, u32[]{:S(2)}) copy-start(bf16[1,64,256]{2,1,0:T(8,128)(2,1)} %get-tuple-element.151) | copy-start | bytes 98308
  529.2 16.5 %copy-start.62 = (f32[16,2,6]{2,1,0:T(2,128)S(1)}, f32[16,2,6]{2,1,0:T(2,128)}, u32[]{:S(2)}) copy-start(f32[16,2,6]{2,1,0:T(2,128)} %copy.387) | copy-start | bytes 2308
  529.2 17.7 %copy-start.65 = (f32[16,2,6]{2,1,0:T(2,128)S(1)}, f32[16,2,6]{2,1,0:T(2,128)}, u32[]{:S(2)}) copy-start(f32[16,2,6]{2,1,0:T(2,128)} %copy.359) | copy-start | bytes 2308
  529.2 18.9 %copy-start.64 = (f32[16,2,6]{2,1,0:T(2,128)S(1)}, f32[16,2,6]{2,1,0:T(2,128)}, u32[]{:S(2)}) copy-start(f32[16,2,6]{2,1,0:T(2,128)} %copy.345) | copy-start | bytes 2308
  537.9 44.0 %copy-start.52 = (bf16[1,64,256]{2,0,1:T(2,128)(2,1)S(1)}, bf16[1,64,256]{2,0,1:T(2,128)(2,1)}, u32[]{:S(2)}) copy-start(bf16[1,64,256]{2,0,1:T(2,128)(2,1)} %copy.395) | copy-start | bytes 98308
  551.3 318.5 %all-reduce.26.cloned.1.call-start = ((), (), s32[]{:S(2)}) async-start(), calls=%async_computation.3 | async-start | bytes 12582912 | tf_op jit(solution)/shard_map/psum | solution.py:171
  585.8 284.0 %copy-start.29 = (bf16[4,64,256]{2,0,1:T(4,128)(2,1)S(1)}, bf16[4,64,256]{2,0,1:T(4,128)(2,1)}, u32[]{:S(2)}) copy-start(bf16[4,64,256]{2,0,1:T(4,128)(2,1)} %copy-done.28) | copy-start | bytes 393220
  585.8 395.1 %all-reduce.30.cloned.1.call-start = ((), (), s32[]{:S(2)}) async-start(), calls=%async_computation.5 | async-start | bytes 1179648
  587.9 283.4 %copy-start.57 = (f32[64,2,6,2]{2,3,1,0:T(2,128)}, f32[64,2,6,2]{2,3,1,0:T(2,128)S(1)}, u32[]{:S(2)}) copy-start(f32[64,2,6,2]{2,3,1,0:T(2,128)S(1)} %get-tuple-element.230) | copy-start | bytes 18436
  878.3 285.2 %all-reduce.28.cloned.1.call-start = ((), (), s32[]{:S(2)}) async-start(), calls=%async_computation.4 | async-start | bytes 1572864
  (62 other events, 354.3 us)
Sparse Core Ops, SparseCore 0:
  98.6 150.4 all-reduce.19
  253.5 98.6 all-reduce.21
  551.4 156.4 all-reduce.23
  713.0 156.7 all-reduce.25
  878.4 102.5 all-reduce.29
  1060.9 102.4 all-reduce.27
where the time goes:
time: 1180 us; the launch traced here: 1170 us
  waiting for transfers between devices  639 us (54%)
  blocking collectives  315 us (27%)
  local copies, waits for them, and re-layouts  95.5 us (8%)
  other arithmetic  53.3 us (5%)
  matrix products  52.6 us (4%)
  between operations  16.6 us (1%)
    psum x3, waiting for transfers between devices, per_device(): lax.psum((all_peak, all_total, all_output), ('req', 'tp'))  337 us
    unnamed x9, waiting for transfers between devices  302 us
    all_gather x4, blocking collectives, per_device(): piece = lax.all_gather(mixed_in, 'tp', axis=0, tiled=True)  102 us
    all_gather x4, blocking collectives, per_device(): lax.all_gather(normed, 'tp', axis=0, tiled=True)  99.2 us
    psum x1, blocking collectives, per_device(): lax.psum((all_peak, all_total, all_output), ('req', 'tp'))  67 us
    all_gather x4, blocking collectives, per_device(): lax.all_gather(queries.reshape(group_rows, attn_width), 'req', axis=0, ti...  46.6 us
  transfers between devices with their start and end apart: 6, of which 6 were waited for; matrix products, arithmetic and copies ran while one was open for 3% of the time, Pallas kernels for 0%

commit v1 on v0

--- a/solution.py
+++ b/solution.py
@@ -8,6 +8,12 @@
 theta_base = 1000000.0
 norm_eps = 1e-06
 masked_score = -1e30
+
+
+def laid_out(tiles, dim):
+    tiles = jnp.moveaxis(tiles, 0, dim)
+    lengths = tiles.shape
+    return tiles.reshape(*lengths[:dim], lengths[dim] * lengths[dim + 1], *lengths[dim + 2 :])
 
 
 def rms_normed(values):
@@ -152,9 +158,20 @@
         )
         gen_keys = gen_keys.at[step].set(new_keys.reshape(group_rows, kv_width))
         gen_values = gen_values.at[step].set(qkv[:, attn_width + kv_width :])
-        every_query = lax.all_gather(
-            queries.reshape(group_rows, attn_width), "req", axis=0, tiled=True
-        )
+        shard = queries.reshape(group_rows, attn_width)
+        devices = lax.axis_size("req")
+        pairs = [(i, (i + 1) % devices) for i in range(devices)]
+        back = [(b, a) for a, b in pairs]
+        lower, upper = ([], [])
+        for step_2 in range(devices - 1):
+            if step_2 % 2 == 0:
+                lower.append(lax.ppermute(lower[-1] if lower else shard, "req", pairs))
+            else:
+                upper.append(lax.ppermute(upper[-1] if upper else shard, "req", back))
+        pieces_2 = jnp.stack([*lower[::-1], shard, *upper])
+        shift = lax.axis_index("req") - len(lower)
+        pieces_2 = pieces_2[(jnp.arange(devices) - shift) % devices]
+        every_query = laid_out(pieces_2, 0)
         part_peak, part_total, part_output = owned_attention(
             every_query,
             cache_keys,

time: 1180 us -> 1170 us (level)
  blocking collectives: 315 us -> 260 us
  waiting for transfers between devices: 639 us -> 672 us
  starting transfers between devices: 0.42 us -> 13 us
    all_gather x4 -> x0, blocking collectives: 46.6 us -> none  [per_device(): lax.all_gather(queries.reshape(group_rows, attn_width), 'req', axis=0, ti...]
    psum x3, waiting for transfers between devices: 337 us -> 358 us  [per_device(): lax.psum((all_peak, all_total, all_output), ('req', 'tp'))]
    ppermute x0 -> x12, waiting for transfers between devices: none -> 12.6 us  [the longest x8 12.6 us: per_device(): lower.append(lax.ppermute(lower[-1] if lower else shard, 'req', pairs))]
    ppermute x0 -> x12, starting transfers between devices: none -> 12.5 us  [the longest x4 8.42 us: per_device(): upper.append(lax.ppermute(upper[-1] if upper else shard, 'req', back))]
  transfers between devices with their start and end apart: 6 -> 18, of which waited for: 6 -> 10; matrix products, arithmetic and copies ran while one was open for 3% -> 9% of each run, Pallas kernels for 0% -> 0%
where the time goes in v1:
time: 1170 us; the launch traced here: 1160 us
  waiting for transfers between devices  672 us (57%)
  blocking collectives  260 us (22%)
  local copies, waits for them, and re-layouts  90 us (8%)
  other arithmetic  54.4 us (5%)
  matrix products  53.7 us (5%)
  between operations  16.6 us (1%)
  starting transfers between devices  13 us (1%)
    psum x3, waiting for transfers between devices, per_device(): lax.psum((all_peak, all_total, all_output), ('req', 'tp'))  358 us
    unnamed x9, waiting for transfers between devices  301 us
    all_gather x4, blocking collectives, per_device(): lax.all_gather(normed, 'tp', axis=0, tiled=True)  99.7 us
    all_gather x4, blocking collectives, per_device(): piece = lax.all_gather(mixed_in, 'tp', axis=0, tiled=True)  95 us
    psum x1, blocking collectives, per_device(): lax.psum((all_peak, all_total, all_output), ('req', 'tp'))  64.9 us
  transfers between devices with their start and end apart: 18, of which 10 were waited for; matrix products, arithmetic and copies ran while one was open for 9% of the time, Pallas kernels for 0%

profile of v1, /device:TPU:1, one launch (start us, length us, event | category | flops | bytes accessed | tf_op | source)
XLA Modules:
  0.0 1159.3 jit_solution(16566262783576145224)
XLA Ops:
  23.6 27.6 %all-gather = bf16[32,2,1536]{2,1,0:T(2,128)(2,1)S(1)} all-gather(bf16[1,2,1536]{2,1,0:T(2,128)(2,1)S(1)} %fusion.170), channel_id=1, replica_groups=mesh['req'=4,'tp'=32] {'tp'}, dimensions={0}, use_global_device_ids=true | all-gather | bytes 202752 | tf_op jit(solution)/shard_map/all_gather | solution.py:146
  51.3 4.0 fusion.28
  68.7 7.0 reshape.1185
  75.7 6.9 reshape.1186
  89.1 6.9 collective-permute-done.1
  115.9 64.9 %all-reduce.9 = (f32[256,2,6]{0,1,2:T(2,128)S(1)}, f32[256,2,6]{0,1,2:T(2,128)S(1)}) all-reduce(f32[256,2,6]{0,1,2:T(2,128)S(1)} %copy.328, f32[256,2,6]{0,1,2:T(2,128)S(1)} %copy.335), channel_id=1, replica_groups=mesh['req'=4,'tp'=32] {'req','tp'}, use_global_device_ids=true, to_apply=%region_6.10 | all-reduce | flops 6144 | bytes 49152 | tf_op jit(solution)/shard_map/psum | solution.py:188
  181.5 72.3 %all-reduce.20.cloned.1.call-done = f32[256,2,6,128]{3,1,2,0:T(2,128)} async-done(((f32[256,2,6,128]{3,1,2,0:T(2,128)}), f32[256,2,6,128]{3,1,2,0:T(2,128)}) %all-reduce.20.cloned.1.call-update) | async-done | bytes 1572880 | tf_op jit(solution)/shard_map/psum | solution.py:188
  258.7 98.2 %all-reduce.22.cloned.1.call-done = bf16[64,1536]{1,0:T(8,128)(2,1)} async-done(((bf16[64,1536]{1,0:T(8,128)(2,1)}), bf16[64,1536]{1,0:T(8,128)(2,1)}) %all-reduce.22.cloned.1.call-update) | async-done | bytes 196624
  359.2 24.5 %all-gather.4 = bf16[32,2,1536]{2,1,0:T(2,128)(2,1)S(1)} all-gather(bf16[1,2,1536]{2,1,0:T(2,128)(2,1)S(1)} %get-tuple-element.172), channel_id=1, replica_groups=mesh['req'=4,'tp'=32] {'tp'}, dimensions={0}, use_global_device_ids=true | all-gather | bytes 202752 | tf_op jit(solution)/shard_map/all_gather | solution.py:146
  383.8 4.0 fusion.30
  388.5 23.3 %all-gather.6 = bf16[32,2,1536]{2,1,0:T(2,128)(2,1)S(1)} all-gather(bf16[1,2,1536]{2,1,0:T(2,128)(2,1)S(1)} %get-tuple-element.173), channel_id=1, replica_groups=mesh['req'=4,'tp'=32] {'tp'}, dimensions={0}, use_global_device_ids=true | all-gather | bytes 202752 | tf_op jit(solution)/shard_map/all_gather | solution.py:146
  411.9 4.0 fusion.31
  420.7 24.3 %all-gather.2 = bf16[32,2,1536]{2,1,0:T(2,128)(2,1)S(1)} all-gather(bf16[1,2,1536]{2,1,0:T(2,128)(2,1)S(1)} %get-tuple-element.171), channel_id=1, replica_groups=mesh['req'=4,'tp'=32] {'tp'}, dimensions={0}, use_global_device_ids=true | all-gather | bytes 202752 | tf_op jit(solution)/shard_map/all_gather | solution.py:146
  445.1 4.0 fusion.29
  480.8 23.5 %all-gather.1 = bf16[32,2,1536]{2,1,0:T(2,128)(2,1)S(1)} all-gather(bf16[1,2,1536]{2,1,0:T(2,128)(2,1)S(1)} %copy-done.47), channel_id=1, replica_groups=mesh['req'=4,'tp'=32] {'tp'}, dimensions={0}, use_global_device_ids=true | all-gather | bytes 202752 | tf_op jit(solution)/shard_map/all_gather | solution.py:222
  524.6 4.0 fusion.208
  546.6 4.1 fusion.73
  564.1 130.8 %all-reduce.24.cloned.1.call-done = (f32[256,2,6]{2,1,0:T(2,128)}, f32[256,2,6]{2,1,0:T(2,128)}, f32[256,2,6]{2,1,0:T(2,128)}, f32[256,2,6]{2,1,0:T(2,128)}, f32[256,2,6]{2,1,0:T(2,128)}, /*index=5*/f32[256,2,6]{2,1,0:T(2,128)}) async-done(((f32[256,2,6]{2,1,0:T(2,128)}, f32[256,2,6]{2,1,0:T(2,128)}, f32[256,2,6]{2,1,0:T(2,128)}, f32[256,2,6]{2,1,0:T(2,128)}, f32[256,2,6]{2,1,0:T(2,128)}, ...) | async-done | bytes 73744 | tf_op jit(solution)/shard_map/psum | solution.py:188
  701.9 154.8 %all-reduce.26.cloned.1.call-done = (f32[256,2,6,128]{3,2,1,0:T(8,128)}, f32[256,2,6,128]{3,2,1,0:T(8,128)}, f32[256,2,6,128]{3,2,1,0:T(8,128)}) async-done(((f32[256,2,6,128]{3,2,1,0:T(8,128)}, f32[256,2,6,128]{3,2,1,0:T(8,128)}, f32[256,2,6,128]{3,2,1,0:T(8,128)}), (f32[256,2,6,128]{3,2,1,0:T(8,128)}, f32[256,2,6,128]{3,2,1,0:T(8,128)}, f32[256,2,6,128]{3,2,1,0:T(8,128)})) %all-reduce.26.cloned.1.call-update) | async-done | bytes 4718608 | tf_op jit(solution)/shard_map/psum | solution.py:188
  867.4 100.5 %all-reduce.30.cloned.1.call-done = (bf16[64,1536]{1,0:T(8,128)(2,1)}, bf16[64,1536]{1,0:T(8,128)(2,1)}, bf16[64,1536]{1,0:T(8,128)(2,1)}) async-done(((bf16[64,1536]{1,0:T(8,128)(2,1)}, bf16[64,1536]{1,0:T(8,128)(2,1)}, bf16[64,1536]{1,0:T(8,128)(2,1)}), (bf16[64,1536]{1,0:T(8,128)(2,1)}, bf16[64,1536]{1,0:T(8,128)(2,1)}, bf16[64,1536]{1,0:T(8,128)(2,1)})) %all-reduce.30.cloned.1.call-update) | async-done | bytes 589840
  969.8 24.9 %all-gather.3 = bf16[32,2,1536]{2,1,0:T(2,128)(2,1)S(1)} all-gather(bf16[1,2,1536]{2,1,0:T(2,128)(2,1)S(1)} %get-tuple-element.174), channel_id=1, replica_groups=mesh['req'=4,'tp'=32] {'tp'}, dimensions={0}, use_global_device_ids=true | all-gather | bytes 202752 | tf_op jit(solution)/shard_map/all_gather | solution.py:222
  996.8 22.5 %all-gather.5 = bf16[32,2,1536]{2,1,0:T(2,128)(2,1)S(1)} all-gather(bf16[1,2,1536]{2,1,0:T(2,128)(2,1)S(1)} %get-tuple-element.176), channel_id=1, replica_groups=mesh['req'=4,'tp'=32] {'tp'}, dimensions={0}, use_global_device_ids=true | all-gather | bytes 202752 | tf_op jit(solution)/shard_map/all_gather | solution.py:222
  1021.5 24.1 %all-gather.7 = bf16[32,2,1536]{2,1,0:T(2,128)(2,1)S(1)} all-gather(bf16[1,2,1536]{2,1,0:T(2,128)(2,1)S(1)} %get-tuple-element.175), channel_id=1, replica_groups=mesh['req'=4,'tp'=32] {'tp'}, dimensions={0}, use_global_device_ids=true | all-gather | bytes 202752 | tf_op jit(solution)/shard_map/all_gather | solution.py:222
  1047.8 102.6 %all-reduce.28.cloned.1.call-done = (bf16[64,1536]{1,0:T(8,128)(2,1)}, bf16[64,1536]{1,0:T(8,128)(2,1)}, bf16[64,1536]{1,0:T(8,128)(2,1)}, bf16[64,1536]{1,0:T(8,128)(2,1)}) async-done(((bf16[64,1536]{1,0:T(8,128)(2,1)}, bf16[64,1536]{1,0:T(8,128)(2,1)}, bf16[64,1536]{1,0:T(8,128)(2,1)}, bf16[64,1536]{1,0:T(8,128)(2,1)}), (bf16[64,1536]{1,0:T(8,128)(2,1)}, bf16[64,1536]{1,0:T(8,128)(2,1)}, ...) | async-done | bytes 786448
  (504 shorter events, 178.9 us)
Async XLA Ops:
  6.5 859.2 %copy-start = (bf16[280,1536]{1,0:T(8,128)(2,1)S(1)}, bf16[280,1536]{1,0:T(8,128)(2,1)}, u32[]{:S(2)}) copy-start(bf16[280,1536]{1,0:T(8,128)(2,1)} %param.42) | copy-start | bytes 2580484
  6.5 247.2 %all-reduce.20.cloned.1.call-start = ((), (), s32[]{:S(2)}) async-start(), calls=%async_computation | async-start | bytes 3145728 | tf_op jit(solution)/shard_map/psum | solution.py:188
  56.3 398.3 %copy-start.33 = (f32[64,64]{1,0:T(8,128)}, f32[64,64]{1,0:T(8,128)S(1)}, u32[]{:S(2)}) copy-start(f32[64,64]{1,0:T(8,128)S(1)} %get-tuple-element.182) | copy-start | bytes 49156
  56.3 398.4 %copy-start.34 = (f32[64,64]{1,0:T(8,128)}, f32[64,64]{1,0:T(8,128)S(1)}, u32[]{:S(2)}) copy-start(f32[64,64]{1,0:T(8,128)S(1)} %get-tuple-element.183) | copy-start | bytes 49156
  56.8 32.1 %collective-permute-start = (bf16[64,1536]{1,0:T(8,128)(2,1)S(1)}, bf16[64,1536]{1,0:T(8,128)(2,1)S(1)}, u32[]{:S(2)}, u32[]{:S(2)}) collective-permute-start(bf16[64,1536]{1,0:T(8,128)(2,1)S(1)} %bitcast.350), channel_id=1, source_target_pairs={{0,32},{32,64},{64,96},{96,0},{1,33},{33,65},{65,97},{97,1},{2,34}... | collective-permute-start | bytes 589832 | tf_op jit(solution)/shard_map/ppermute | solution.py:168
  58.0 31.1 %collective-permute-start.2 = (bf16[64,1536]{1,0:T(8,128)(2,1)S(1)}, bf16[64,1536]{1,0:T(8,128)(2,1)S(1)}, u32[]{:S(2)}, u32[]{:S(2)}) collective-permute-start(bf16[64,1536]{1,0:T(8,128)(2,1)S(1)} %bitcast.351), channel_id=1, source_target_pairs={{32,0},{64,32},{96,64},{0,96},{33,1},{65,33},{97,65},{1,97},{34,2}... | collective-permute-start | bytes 589832 | tf_op jit(solution)/shard_map/ppermute | solution.py:170
  88.8 7.2 collective-permute-start.1
  106.2 250.6 %all-reduce.22.cloned.1.call-start = ((), (), s32[]{:S(2)}) async-start(), calls=%async_computation.1 | async-start | bytes 393216
  110.2 146.8 %copy-start.10 = (bf16[48,1536]{1,0:T(8,128)(2,1)S(1)}, bf16[48,1536]{1,0:T(8,128)(2,1)}, u32[]{:S(2)}) copy-start(bf16[48,1536]{1,0:T(8,128)(2,1)} %param.39) | copy-start | bytes 442372
  258.0 436.9 %all-reduce.24.cloned.1.call-start = ((), (), s32[]{:S(2)}) async-start(), calls=%async_computation.2 | async-start | bytes 3145728 | tf_op jit(solution)/shard_map/psum | solution.py:188
  417.1 87.2 %collective-permute-start.9 = (bf16[64,1536]{1,0:T(8,128)(2,1)}, bf16[64,1536]{1,0:T(8,128)(2,1)}, u32[]{:S(2)}, u32[]{:S(2)}) collective-permute-start(bf16[64,1536]{1,0:T(8,128)(2,1)} %bitcast.304), channel_id=1, source_target_pairs={{0,32},{32,64},{64,96},{96,0},{1,33},{33,65},{65,97},{97,1},{2,34}... | collective-permute-start | bytes 589832 | tf_op jit(solution)/shard_map/ppermute | solution.py:168
  418.3 89.0 %collective-permute-start.11 = (bf16[64,1536]{1,0:T(8,128)(2,1)}, bf16[64,1536]{1,0:T(8,128)(2,1)}, u32[]{:S(2)}, u32[]{:S(2)}) collective-permute-start(bf16[64,1536]{1,0:T(8,128)(2,1)} %bitcast.304), channel_id=1, source_target_pairs={{32,0},{64,32},{96,64},{0,96},{33,1},{65,33},{97,65},{1,97},{34,2}... | collective-permute-start | bytes 589832 | tf_op jit(solution)/shard_map/ppermute | solution.py:170
  451.0 59.1 %collective-permute-start.3 = (bf16[64,1536]{1,0:T(8,128)(2,1)}, bf16[64,1536]{1,0:T(8,128)(2,1)}, u32[]{:S(2)}, u32[]{:S(2)}) collective-permute-start(bf16[64,1536]{1,0:T(8,128)(2,1)} %bitcast.306), channel_id=1, source_target_pairs={{0,32},{32,64},{64,96},{96,0},{1,33},{33,65},{65,97},{97,1},{2,34}... | collective-permute-start | bytes 589832 | tf_op jit(solution)/shard_map/ppermute | solution.py:168
  451.0 64.2 %collective-permute-start.5 = (bf16[64,1536]{1,0:T(8,128)(2,1)}, bf16[64,1536]{1,0:T(8,128)(2,1)}, u32[]{:S(2)}, u32[]{:S(2)}) collective-permute-start(bf16[64,1536]{1,0:T(8,128)(2,1)} %bitcast.306), channel_id=1, source_target_pairs={{32,0},{64,32},{96,64},{0,96},{33,1},{65,33},{97,65},{1,97},{34,2}... | collective-permute-start | bytes 589832 | tf_op jit(solution)/shard_map/ppermute | solution.py:170
  470.2 39.9 %collective-permute-start.6 = (bf16[64,1536]{1,0:T(8,128)(2,1)}, bf16[64,1536]{1,0:T(8,128)(2,1)}, u32[]{:S(2)}, u32[]{:S(2)}) collective-permute-start(bf16[64,1536]{1,0:T(8,128)(2,1)} %bitcast.305), channel_id=1, source_target_pairs={{0,32},{32,64},{64,96},{96,0},{1,33},{33,65},{65,97},{97,1},{2,34}... | collective-permute-start | bytes 589832 | tf_op jit(solution)/shard_map/ppermute | solution.py:168
  504.4 8.3 collective-permute-start.10
  507.3 12.9 %collective-permute-start.8 = (bf16[64,1536]{1,0:T(8,128)(2,1)}, bf16[64,1536]{1,0:T(8,128)(2,1)}, u32[]{:S(2)}, u32[]{:S(2)}) collective-permute-start(bf16[64,1536]{1,0:T(8,128)(2,1)} %bitcast.305), channel_id=1, source_target_pairs={{32,0},{64,32},{96,64},{0,96},{33,1},{65,33},{97,65},{1,97},{34,2}... | collective-permute-start | bytes 589832 | tf_op jit(solution)/shard_map/ppermute | solution.py:170
  510.2 7.5 collective-permute-start.4
  510.2 11.7 %collective-permute-start.7 = (bf16[64,1536]{1,0:T(8,128)(2,1)}, bf16[64,1536]{1,0:T(8,128)(2,1)}, u32[]{:S(2)}, u32[]{:S(2)}) collective-permute-start(bf16[64,1536]{1,0:T(8,128)(2,1)} %collective-permute-done.6), channel_id=1, source_target_pairs={{0,32},{32,64},{64,96},{96,0},{1,33},{33,65},{65,97},{97,1},{2,34}... | collective-permute-start | bytes 589832 | tf_op jit(solution)/shard_map/ppermute | solution.py:168
  546.3 310.5 %all-reduce.26.cloned.1.call-start = ((), (), s32[]{:S(2)}) async-start(), calls=%async_computation.3 | async-start | bytes 12582912 | tf_op jit(solution)/shard_map/psum | solution.py:188
  561.6 295.1 %copy-start.30 = (bf16[4,64,256]{2,0,1:T(4,128)(2,1)S(1)}, bf16[4,64,256]{2,0,1:T(4,128)(2,1)}, u32[]{:S(2)}) copy-start(bf16[4,64,256]{2,0,1:T(4,128)(2,1)} %copy-done.29) | copy-start | bytes 393220
  561.7 406.3 %all-reduce.30.cloned.1.call-start = ((), (), s32[]{:S(2)}) async-start(), calls=%async_computation.5 | async-start | bytes 1179648
  563.2 295.2 %copy-start.45 = (f32[64,2,6,2]{2,3,1,0:T(2,128)}, f32[64,2,6,2]{2,3,1,0:T(2,128)S(1)}, u32[]{:S(2)}) copy-start(f32[64,2,6,2]{2,3,1,0:T(2,128)S(1)} %get-tuple-element.230) | copy-start | bytes 18436
  865.3 285.1 %all-reduce.28.cloned.1.call-start = ((), (), s32[]{:S(2)}) async-start(), calls=%async_computation.4 | async-start | bytes 1572864
  (58 other events, 533.9 us)
Sparse Core Ops, SparseCore 0:
  106.4 147.3 all-reduce.19
  258.1 98.6 all-reduce.21
  546.4 148.4 all-reduce.23
  700.0 156.7 all-reduce.25
  865.4 102.4 all-reduce.29
  1047.9 102.4 all-reduce.27
